TPU v7x, 32 devices: a whole 2x2x4 slice. The times are simulated.
32 devices in a mesh: dp: 8 (over z, y), rep: 4 (over x, core).
Axes of the slice: x: 2, y: 2, z: 4, core: 2. Of those that a mesh axis runs over, the one named last changes fastest.
Arguments:
- circuits: bfloat16 [8192, 1024], P(('dp', 'rep')), may hold values from -2.65 to 2.65
- records: bfloat16 [8192, 1024], P(('dp', 'rep')), may hold values from -0.25 to 0.25
- record_gain: float32 [1024], replicated, may hold values from 0.5 to 2
- log_scale: float32 [1], replicated, may hold values from 1.6 to 2.4
- logit_bias: float32 [1], replicated, may hold values from -3 to -1
- hard_ids: int32 [8192, 16], P(('dp', 'rep')), may hold values from -1 to 8191, as said below
Outputs:
- grad_circuits: float32 [8192, 1024], P(('dp', 'rep'))
- grad_records: float32 [8192, 1024], P(('dp', 'rep'))
- grad_gain: float32 [1024], replicated
- statistics: float32 [2], replicated
- mean_loss: float32 [1], replicated
Inputs may be any that keep to these rules, and one draw needn't show every extreme that they name: `hard_ids`: every entry that is not -1 names a row held by a device with the same dp index as the pair's device (the same value of row // 1024). Over the 256 pairs of one device, at most 16 entries name rows of any one device, and in each dp index one device is named exactly 16 times by every device of that dp index.
All inputs are finite; a program needn't handle non-finite values.
Results may differ from a plain program's by a relative error of at most 0.0043.
Values may be sent and summed in bfloat16 or wider, within the bound.
A program may use at most 64 MiB of HBM per device.

v0:
```python
import jax
import jax.numpy as jnp
from jax import lax
from jax.sharding import PartitionSpec as P

HOPS = 4
EPSILON = 1e-06


def shifted(value, axis, steps):
    count = lax.axis_size(axis)
    pairs = [(source, (source + steps) % count) for source in range(count)]
    return lax.ppermute(value, axis, pairs)


def unit_rows(values):
    sq_total = jnp.sum(values * values, axis=-1, keepdims=True)
    lengths = jnp.sqrt(sq_total + EPSILON)
    return (values / lengths, lengths)


def transposed_product(left, right):
    return lax.dot_general(
        left, right, (((0,), (0,)), ((), ())), preferred_element_type=jnp.float32
    )


def score_tile(circ_block, rec_block, multiplier, bias_value, own_block):
    products = lax.dot_general(
        circ_block, rec_block, (((1,), (1,)), ((), ())), preferred_element_type=jnp.float32
    )
    scores = products * multiplier + bias_value
    weights = jax.nn.sigmoid(scores)
    losses = jax.nn.softplus(scores)
    if own_block:
        tile_rows = scores.shape[0]
        diag_mask = (
            lax.broadcasted_iota(jnp.int32, (tile_rows, tile_rows), 0)
            == lax.broadcasted_iota(jnp.int32, (tile_rows, tile_rows), 1)
        ).astype(jnp.float32)
        weights = weights - diag_mask
        losses = losses - scores * diag_mask
    summary = jnp.stack(
        [jnp.sum(weights * (scores - bias_value)), jnp.sum(weights), jnp.sum(losses)]
    )
    return (weights.astype(jnp.bfloat16), summary)


def tile_terms(circ_block, rec_block, multiplier, bias_value):
    products = lax.dot_general(
        circ_block, rec_block, (((1,), (1,)), ((), ())), preferred_element_type=jnp.float32
    )
    return products * multiplier + bias_value


def per_device(circuits, records, record_gain, log_scale, logit_bias, hard_ids):
    pair_rows = circuits.shape[0]
    list_width = hard_ids.shape[1]
    rep_count = lax.axis_size("rep")
    loop_count = lax.axis_size("dp")
    circ_unit, circ_length = unit_rows(circuits.astype(jnp.float32))
    circ_emb = circ_unit.astype(jnp.bfloat16)
    rec_pre = records.astype(jnp.float32) * record_gain
    rec_unit, rec_length = unit_rows(rec_pre)
    rec_emb = rec_unit.astype(jnp.bfloat16)
    multiplier = jnp.exp(log_scale[0])
    bias_value = logit_bias[0]
    even = lax.axis_index("dp") % 2 == 0
    swap = [(source, source ^ 1) for source in range(loop_count)]
    rec2 = shifted(rec_emb, "dp", -2)
    circ2 = shifted(circ_emb, "dp", 2)
    rec4 = shifted(rec2, "dp", -2)
    circ4 = shifted(circ2, "dp", 2)
    rec1 = lax.ppermute(jnp.where(even, rec2, rec_emb), "dp", swap)
    circ1 = lax.ppermute(jnp.where(even, circ_emb, circ2), "dp", swap)
    rec3 = lax.ppermute(jnp.where(even, rec4, rec2), "dp", swap)
    circ3 = lax.ppermute(jnp.where(even, circ2, circ4), "dp", swap)
    own_weights, summary = score_tile(circ_emb, rec_emb, multiplier, bias_value, True)
    grad_circ = jnp.dot(own_weights, rec_emb, preferred_element_type=jnp.float32)
    grad_rec = transposed_product(own_weights, circ_emb)
    everyone = lax.all_gather(rec_emb, "rep", axis=0, tiled=True)
    first_row = lax.axis_index("dp") * rep_count * pair_rows
    columns = lax.broadcasted_iota(jnp.int32, (pair_rows, rep_count * pair_rows), 1) + first_row
    times = jnp.zeros(columns.shape, jnp.float32)
    for entry in range(list_width):
        times = times + (hard_ids[:, entry][:, None] == columns).astype(jnp.float32)
    for visitor, guest in ((rec2, circ2), (rec1, circ1), (rec4, circ4), (rec3, circ3)):
        weights, portion = score_tile(circ_emb, visitor, multiplier, bias_value, False)
        grad_circ = grad_circ + jnp.dot(weights, visitor, preferred_element_type=jnp.float32)
        summary = summary + portion
        scores = tile_terms(guest, rec_emb, multiplier, bias_value)
        weights = jax.nn.sigmoid(scores).astype(jnp.bfloat16)
        grad_rec = grad_rec + transposed_product(weights, guest)
    scores = tile_terms(circ_emb, everyone, multiplier, bias_value)
    sigmoids = jax.nn.sigmoid(scores)
    weights = times * sigmoids
    narrow = (times * sigmoids.astype(jnp.bfloat16).astype(jnp.float32)).astype(jnp.bfloat16)
    hard_grad = jnp.dot(narrow, everyone, preferred_element_type=jnp.float32)
    summary = summary + jnp.stack(
        [
            jnp.sum(weights * (scores - bias_value)),
            jnp.sum(weights),
            jnp.sum(times * jax.nn.softplus(scores)),
        ]
    )
    grad_circ_emb = multiplier * (grad_circ + hard_grad)
    grad_rec_emb = multiplier * grad_rec
    grad_circuits = (
        grad_circ_emb - circ_unit * jnp.sum(circ_unit * grad_circ_emb, axis=-1, keepdims=True)
    ) / circ_length
    grad_pre = (
        grad_rec_emb - rec_unit * jnp.sum(rec_unit * grad_rec_emb, axis=-1, keepdims=True)
    ) / rec_length
    grad_records = grad_pre * record_gain
    gain_part = jnp.sum(records.astype(jnp.float32) * grad_pre, axis=0)
    gain_total, summary_total = lax.psum((gain_part, summary), ("dp", "rep"))
    pair_total = pair_rows * loop_count * rep_count
    statistics = jnp.stack([summary_total[0], summary_total[1]])
    mean_loss = jnp.stack([summary_total[2] / pair_total])
    return (grad_circuits, grad_records, gain_total, statistics, mean_loss)


def solution(mesh):
    placed = (P(("dp", "rep"), None), P(("dp", "rep"), None), P(), P(), P(), P(("dp", "rep"), None))
    return jax.shard_map(
        per_device,
        mesh=mesh,
        in_specs=placed,
        out_specs=(P(("dp", "rep"), None), P(("dp", "rep"), None), P(), P(), P()),
        check_vma=False,
    )
```

profile of v0, /device:TPU:0, one launch (start us, length us, event | category | flops | bytes accessed | tf_op | source)
XLA Modules:
  0.0 178.6 jit_solution(16136791953172690187)
XLA Ops:
  8.6 2.0 %fusion.84 = bf16[256,1024]{1,0:T(8,128)(2,1)} fusion(f32[256]{0:T(256)S(1)} %add_sqrt_fusion, f32[1024]{0:T(1024)} %param.8, bf16[256,1024]{1,0:T(8,128)(2,1)} %param.7), kind=kLoop, calls=%fused_computation.140 | loop fusion | flops 1048576 | bytes 1053696 | tf_op jit(solution)/shard_map/convert_element_type | solution.py:65
  10.6 5.1 %collective-permute-start = (bf16[256,1024]{1,0:T(8,128)(2,1)}, bf16[256,1024]{1,0:T(8,128)(2,1)}, u32[]{:S(2)}, u32[]{:S(2)}) collective-permute-start(bf16[256,1024]{1,0:T(8,128)(2,1)} %fusion.84), channel_id=1, source_target_pairs={{0,24},{4,28},{8,0},{12,4},{16,8},{20,12},{24,16},{28,20},{1,25},{... | collective-permute-start | bytes 1572872 | tf_op jit(solution)/shard_map/ppermute | solution.py:13
  20.5 7.8 %collective-permute-done = bf16[256,1024]{1,0:T(8,128)(2,1)} collective-permute-done((bf16[256,1024]{1,0:T(8,128)(2,1)}, bf16[256,1024]{1,0:T(8,128)(2,1)}, u32[]{:S(2)}, u32[]{:S(2)}) %collective-permute-start) | collective-permute-done | bytes 524320 | tf_op jit(solution)/shard_map/ppermute | solution.py:13
  28.4 4.3 %collective-permute-start.2 = (bf16[256,1024]{1,0:T(8,128)(2,1)}, bf16[256,1024]{1,0:T(8,128)(2,1)}, u32[]{:S(2)}, u32[]{:S(2)}) collective-permute-start(bf16[256,1024]{1,0:T(8,128)(2,1)} %collective-permute-done), channel_id=1, source_target_pairs={{0,24},{4,28},{8,0},{12,4},{16,8},{20,12},{24,16},{28,20},{1,25},{... | collective-permute-start | bytes 1572872 | tf_op jit(solution)/shard_map/ppermute | solution.py:13
  32.6 7.8 %collective-permute-done.4 = bf16[256,1024]{1,0:T(8,128)(2,1)S(1)} collective-permute-done((bf16[256,1024]{1,0:T(8,128)(2,1)S(1)}, bf16[256,1024]{1,0:T(8,128)(2,1)S(1)}, u32[]{:S(2)}, u32[]{:S(2)}) %collective-permute-start.4) | collective-permute-done | bytes 524320 | tf_op jit(solution)/shard_map/ppermute | solution.py:13
  42.0 3.1 %convolution_add_fusion.2 = f32[256,1024]{1,0:T(8,128)} fusion(f32[256,1024]{1,0:T(8,128)} %fusion.68, bf16[256,1024]{1,0:T(8,128)(2,1)S(1)} %collective-permute-done.4, bf16[256,1024]{1,0:T(8,128)(2,1)S(1)} %copy-done, f32[]{:T(128)} %bitcast.69, f32[]{:T(128)} %bitcast), kind=kOutput, calls=%fused_computation.5 | convolution fusion | flops 269090816 | bytes 3145736 | tf_op jit(solution)/shard_map/dot_general | solution.py:23
  45.1 2.2 %multiply_reduce_fusion.7 = (f32[]{:T(128)}, f32[]{:T(128)}, f32[]{:T(128)}, f32[256,256]{1,0:T(8,128)S(1)}) fusion(f32[]{:T(128)} %bitcast.74, f32[]{:T(128)} %bitcast, bf16[256,1024]{1,0:T(8,128)(2,1)S(1)} %fusion.83, bf16[256,1024]{1,0:T(8,128)(2,1)} %collective-permute-done), kind=kOutput, calls=%fused_computation.94 | convolution fusion | flops 135266304 | bytes 1310740 | tf_op jit(solution)/shard_map/dot_general | solution.py:29
  47.3 2.4 %convolution_add_fusion.5 = f32[256,1024]{1,0:T(8,128)} fusion(f32[256,1024]{1,0:T(8,128)S(1)} %fusion.70, bf16[256,1024]{1,0:T(8,128)(2,1)} %collective-permute-done, f32[256,256]{1,0:T(8,128)S(1)} %get-tuple-element.55), kind=kOutput, calls=%fused_computation.11 | convolution fusion | flops 134742016 | bytes 2883584 | tf_op jit(solution)/shard_map/dot_general | solution.py:89
  49.7 1.9 %collective-permute-done.2 = bf16[256,1024]{1,0:T(8,128)(2,1)} collective-permute-done((bf16[256,1024]{1,0:T(8,128)(2,1)}, bf16[256,1024]{1,0:T(8,128)(2,1)}, u32[]{:S(2)}, u32[]{:S(2)}) %collective-permute-start.2) | collective-permute-done | bytes 524320 | tf_op jit(solution)/shard_map/ppermute | solution.py:13
  51.6 1.6 broadcast_select_fusion.3
  55.3 6.6 %collective-permute-done.6 = bf16[256,1024]{1,0:T(8,128)(2,1)} collective-permute-done((bf16[256,1024]{1,0:T(8,128)(2,1)S(1)}, bf16[256,1024]{1,0:T(8,128)(2,1)}, u32[]{:S(2)}, u32[]{:S(2)}) %collective-permute-start.6) | collective-permute-done | bytes 524320 | tf_op jit(solution)/shard_map/ppermute | solution.py:13
  63.0 2.6 %collective-permute-start.7 = (bf16[256,1024]{1,0:T(8,128)(2,1)S(1)}, bf16[256,1024]{1,0:T(8,128)(2,1)S(1)}, u32[]{:S(2)}, u32[]{:S(2)}) collective-permute-start(bf16[256,1024]{1,0:T(8,128)(2,1)S(1)} %get-tuple-element.28), channel_id=1, source_target_pairs={{0,4},{4,0},{8,12},{12,8},{16,20},{20,16},{24,28},{28,24},{1,5},{5... | collective-permute-start | bytes 1572872 | tf_op jit(solution)/shard_map/ppermute | solution.py:77
  65.6 2.9 %multiply_reduce_fusion.5 = (f32[]{:T(128)}, f32[]{:T(128)}, f32[]{:T(128)}, f32[256,256]{1,0:T(8,128)}) fusion(f32[]{:T(128)} %bitcast.72, f32[]{:T(128)} %bitcast, bf16[256,1024]{1,0:T(8,128)(2,1)S(1)} %copy-done.6, bf16[256,1024]{1,0:T(8,128)(2,1)} %collective-permute-done.2), kind=kOutput, calls=%fused_computation.92 | convolution fusion | flops 135266304 | bytes 1310740 | tf_op jit(solution)/shard_map/dot_general | solution.py:29
  71.0 8.3 %collective-permute-done.1 = bf16[256,1024]{1,0:T(8,128)(2,1)S(1)} collective-permute-done((bf16[256,1024]{1,0:T(8,128)(2,1)S(1)}, bf16[256,1024]{1,0:T(8,128)(2,1)S(1)}, u32[]{:S(2)}, u32[]{:S(2)}) %collective-permute-start.1) | collective-permute-done | bytes 524320 | tf_op jit(solution)/shard_map/ppermute | solution.py:74
  80.5 10.0 %collective-permute-done.7 = bf16[256,1024]{1,0:T(8,128)(2,1)S(1)} collective-permute-done((bf16[256,1024]{1,0:T(8,128)(2,1)S(1)}, bf16[256,1024]{1,0:T(8,128)(2,1)S(1)}, u32[]{:S(2)}, u32[]{:S(2)}) %collective-permute-start.7) | collective-permute-done | bytes 524320 | tf_op jit(solution)/shard_map/ppermute | solution.py:77
  91.3 3.1 %fusion.37 = f32[256,1024]{1,0:T(8,128)} fusion(bf16[256,1024]{1,0:T(8,128)(2,1)} %copy-done.13, bf16[256,1024]{1,0:T(8,128)(2,1)S(1)} %copy-done, f32[]{:T(128)} %bitcast.76, f32[]{:T(128)} %bitcast), kind=kOutput, calls=%fused_computation.58 | convolution fusion | flops 268828672 | bytes 2097160 | tf_op jit(solution)/shard_map/dot_general | solution.py:23
  94.4 6.1 %collective-permute-done.5 = bf16[256,1024]{1,0:T(8,128)(2,1)S(1)} collective-permute-done((bf16[256,1024]{1,0:T(8,128)(2,1)}, bf16[256,1024]{1,0:T(8,128)(2,1)S(1)}, u32[]{:S(2)}, u32[]{:S(2)}) %collective-permute-start.5) | collective-permute-done | bytes 524320 | tf_op jit(solution)/shard_map/ppermute | solution.py:75
  100.5 1.9 %convolution_add_fusion.1 = f32[256,1024]{1,0:T(8,128)} fusion(f32[256,1024]{1,0:T(8,128)S(1)} %copy-done.4, bf16[256,1024]{1,0:T(8,128)(2,1)S(1)} %collective-permute-done.5, bf16[256,1024]{1,0:T(8,128)(2,1)S(1)} %copy-done, f32[]{:T(128)} %bitcast.68, f32[]{:T(128)} %bitcast), kind=kOutput, calls=%fused_computation.4 | convolution fusion | flops 269090816 | bytes 3145736 | tf_op jit(solution)/shard_map/dot_general | solution.py:23
  102.4 2.9 %multiply_reduce_fusion.1 = (f32[256]{0:T(256)S(1)}, f32[256,1024]{1,0:T(8,128)S(1)}) fusion(f32[256]{0:T(256)S(1)} %add_sqrt_fusion, f32[1024]{0:T(1024)S(1)} %copy-done.11, bf16[256,1024]{1,0:T(8,128)(2,1)S(1)} %copy-done.1, f32[256,1024]{1,0:T(8,128)} %fusion.37, f32[256,1024]{1,0:T(8,128)} %convolution_add_fusion.1, ...), kind=kOutput, calls=%fused_computation.66 | convolution fusion | flops 270925568 | bytes 4724744 | tf_op jit(solution)/shard_map/dot_general | solution.py:23
  107.1 5.2 %multiply_reduce_fusion = (f32[]{:T(128)}, f32[]{:T(128)}, f32[]{:T(128)}, f32[256,1024]{1,0:T(8,128)S(1)}) fusion(f32[]{:T(128)} %bitcast.70, s32[256]{0:T(256)S(1)} %bitcast.106, s32[256]{0:T(256)S(1)} %bitcast.108, s32[256]{0:T(256)S(1)} %bitcast.80, s32[256]{0:T(256)S(1)} %bitcast.82, s32[256]{0:T(256)S(1)} %bitcast.84, s32[256]{0:T(256)S(1)} %bitcast.86, ...), kind=kOutput, calls=%fused_computation.64 | convolution fusion | flops 553910272 | bytes 3690516 | tf_op jit(solution)/shard_map/dot_general | solution.py:50
  112.3 11.1 %fusion.74 = f32[3]{0:T(128)S(1)} fusion(f32[1]{0:T(128)} %bitcast.32, f32[1]{0:T(128)} %bitcast.31, f32[1]{0:T(128)} %bitcast.30, f32[1]{0:T(128)} %bitcast.35, f32[1]{0:T(128)} %bitcast.34, f32[1]{0:T(128)} %bitcast.33, f32[1]{0:T(128)} %bitcast.29, f32[1]{0:T(128)} %bitcast.28, f32[1]{0:T(128)} %bitcast.27, f32[1]{0:T(128)} %bitcast.26, f32[1]{0:T(128)} %bitcast.25, ...), kind=kLoop, calls=%fused_computation.130 | loop fusion | flops 51 | bytes 84 | tf_op jit(solution)/shard_map/add | solution.py:99
  123.4 39.1 %all-reduce = (f32[1024]{0:T(1024)}, f32[3]{0:T(128)S(1)}) all-reduce(f32[1024]{0:T(1024)S(1)} %get-tuple-element.25, f32[3]{0:T(128)S(1)} %fusion.74), channel_id=1, replica_groups=mesh['dp'=8,'rep'=4] {'dp','rep'}, use_global_device_ids=true, to_apply=%region_5.6 | all-reduce | flops 1027 | bytes 8216 | tf_op jit(solution)/shard_map/psum | solution.py:116
  163.1 4.0 %fusion.43 = f32[256,1024]{1,0:T(8,128)S(1)} fusion(bf16[1024,1024]{1,0:T(8,128)(2,1)} %all-gather.2.cloned.1.call-done, f32[256,1024]{1,0:T(8,128)S(1)} %get-tuple-element.52, s32[1024]{0:T(1024)S(1)} %iota_add_fusion, s32[256]{0:T(256)S(1)} %bitcast.107, s32[256]{0:T(256)S(1)} %bitcast.109, s32[256]{0:T(256)S(1)} %bitcast.81, s32[256]{0:T(256)S(1)} %bitcast.83, ...), kind=kOutput, calls=%fused_computation.77 | convolution fusion | flops 551026688 | bytes 4214784 | tf_op jit(solution)/shard_map/dot_general | solution.py:98
  167.2 1.6 multiply_reduce_fusion.2
  (60 shorter events, 17.7 us)
Async XLA Ops:
  7.2 8.6 %copy-start.2 = (bf16[256,1024]{1,0:T(8,128)(2,1)S(1)}, bf16[256,1024]{1,0:T(8,128)(2,1)}, u32[]{:S(2)}) copy-start(bf16[256,1024]{1,0:T(8,128)(2,1)} %param.6) | copy-start | bytes 1572868
  7.2 9.7 %copy-start.12 = (s32[256,16]{0,1:T(8,128)S(1)}, s32[256,16]{0,1:T(8,128)}, u32[]{:S(2)}) copy-start(s32[256,16]{0,1:T(8,128)} %param.11) | copy-start | bytes 49156
  7.2 99.9 %all-gather.2.cloned.1.call-start = ((), (), s32[]{:S(2)}) async-start(), calls=%async_computation | async-start | bytes 2621440 | tf_op jit(solution)/shard_map/all_gather | solution.py:81
  10.6 7.1 %copy-start = (bf16[256,1024]{1,0:T(8,128)(2,1)S(1)}, bf16[256,1024]{1,0:T(8,128)(2,1)}, u32[]{:S(2)}) copy-start(bf16[256,1024]{1,0:T(8,128)(2,1)} %fusion.84) | copy-start | bytes 1572868
  10.6 17.7 %collective-permute-start = (bf16[256,1024]{1,0:T(8,128)(2,1)}, bf16[256,1024]{1,0:T(8,128)(2,1)}, u32[]{:S(2)}, u32[]{:S(2)}) collective-permute-start(bf16[256,1024]{1,0:T(8,128)(2,1)} %fusion.84), channel_id=1, source_target_pairs={{0,24},{4,28},{8,0},{12,4},{16,8},{20,12},{24,16},{28,20},{1,25},{... | collective-permute-start | bytes 1572872 | tf_op jit(solution)/shard_map/ppermute | solution.py:13
  16.1 28.9 %copy-start.5 = (bf16[256,1024]{1,0:T(8,128)(2,1)}, bf16[256,1024]{1,0:T(8,128)(2,1)S(1)}, u32[]{:S(2)}) copy-start(bf16[256,1024]{1,0:T(8,128)(2,1)S(1)} %fusion.83) | copy-start | bytes 1572868
  16.2 24.3 %collective-permute-start.4 = (bf16[256,1024]{1,0:T(8,128)(2,1)S(1)}, bf16[256,1024]{1,0:T(8,128)(2,1)S(1)}, u32[]{:S(2)}, u32[]{:S(2)}) collective-permute-start(bf16[256,1024]{1,0:T(8,128)(2,1)S(1)} %fusion.83), channel_id=1, source_target_pairs={{0,8},{4,12},{8,16},{12,20},{16,24},{20,28},{24,0},{28,4},{1,9},{5... | collective-permute-start | bytes 1572872 | tf_op jit(solution)/shard_map/ppermute | solution.py:13
  28.4 23.2 %collective-permute-start.2 = (bf16[256,1024]{1,0:T(8,128)(2,1)}, bf16[256,1024]{1,0:T(8,128)(2,1)}, u32[]{:S(2)}, u32[]{:S(2)}) collective-permute-start(bf16[256,1024]{1,0:T(8,128)(2,1)} %collective-permute-done), channel_id=1, source_target_pairs={{0,24},{4,28},{8,0},{12,4},{16,8},{20,12},{24,16},{28,20},{1,25},{... | collective-permute-start | bytes 1572872 | tf_op jit(solution)/shard_map/ppermute | solution.py:13
  40.4 21.4 %collective-permute-start.6 = (bf16[256,1024]{1,0:T(8,128)(2,1)S(1)}, bf16[256,1024]{1,0:T(8,128)(2,1)}, u32[]{:S(2)}, u32[]{:S(2)}) collective-permute-start(bf16[256,1024]{1,0:T(8,128)(2,1)S(1)} %collective-permute-done.4), channel_id=1, source_target_pairs={{0,8},{4,12},{8,16},{12,20},{16,24},{20,28},{24,0},{28,4},{1,9},{5... | collective-permute-start | bytes 1572872 | tf_op jit(solution)/shard_map/ppermute | solution.py:13
  47.3 4.3 %copy-start.1 = (bf16[256,1024]{1,0:T(8,128)(2,1)S(1)}, bf16[256,1024]{1,0:T(8,128)(2,1)}, u32[]{:S(2)}) copy-start(bf16[256,1024]{1,0:T(8,128)(2,1)} %param.7) | copy-start | bytes 1572868
  47.3 4.3 %copy-start.11 = (f32[1024]{0:T(1024)S(1)}, f32[1024]{0:T(1024)}, u32[]{:S(2)}) copy-start(f32[1024]{0:T(1024)} %param.8) | copy-start | bytes 12292
  49.7 16.0 %copy-start.6 = (bf16[256,1024]{1,0:T(8,128)(2,1)S(1)}, bf16[256,1024]{1,0:T(8,128)(2,1)}, u32[]{:S(2)}) copy-start(bf16[256,1024]{1,0:T(8,128)(2,1)} %copy-done.5) | copy-start | bytes 1572868
  53.2 15.4 %collective-permute-start.3 = (bf16[256,1024]{1,0:T(8,128)(2,1)S(1)}, bf16[256,1024]{1,0:T(8,128)(2,1)S(1)}, u32[]{:S(2)}, u32[]{:S(2)}) collective-permute-start(bf16[256,1024]{1,0:T(8,128)(2,1)S(1)} %get-tuple-element.30), channel_id=1, source_target_pairs={{0,4},{4,0},{8,12},{12,8},{16,20},{20,16},{24,28},{28,24},{1,5},{5... | collective-permute-start | bytes 1572872 | tf_op jit(solution)/shard_map/ppermute | solution.py:76
  54.6 24.7 %collective-permute-start.1 = (bf16[256,1024]{1,0:T(8,128)(2,1)S(1)}, bf16[256,1024]{1,0:T(8,128)(2,1)S(1)}, u32[]{:S(2)}, u32[]{:S(2)}) collective-permute-start(bf16[256,1024]{1,0:T(8,128)(2,1)S(1)} %get-tuple-element.29), channel_id=1, source_target_pairs={{0,4},{4,0},{8,12},{12,8},{16,20},{20,16},{24,28},{28,24},{1,5},{5... | collective-permute-start | bytes 1572872 | tf_op jit(solution)/shard_map/ppermute | solution.py:74
  63.0 27.5 %collective-permute-start.7 = (bf16[256,1024]{1,0:T(8,128)(2,1)S(1)}, bf16[256,1024]{1,0:T(8,128)(2,1)S(1)}, u32[]{:S(2)}, u32[]{:S(2)}) collective-permute-start(bf16[256,1024]{1,0:T(8,128)(2,1)S(1)} %get-tuple-element.28), channel_id=1, source_target_pairs={{0,4},{4,0},{8,12},{12,8},{16,20},{20,16},{24,28},{28,24},{1,5},{5... | collective-permute-start | bytes 1572872 | tf_op jit(solution)/shard_map/ppermute | solution.py:77
  65.6 34.9 %collective-permute-start.5 = (bf16[256,1024]{1,0:T(8,128)(2,1)}, bf16[256,1024]{1,0:T(8,128)(2,1)S(1)}, u32[]{:S(2)}, u32[]{:S(2)}) collective-permute-start(bf16[256,1024]{1,0:T(8,128)(2,1)} %get-tuple-element.27), channel_id=1, source_target_pairs={{0,4},{4,0},{8,12},{12,8},{16,20},{20,16},{24,28},{28,24},{1,5},{5... | collective-permute-start | bytes 1572872 | tf_op jit(solution)/shard_map/ppermute | solution.py:75
  79.3 1.2 copy-start.9
  80.5 20.0 %copy-start.4 = (f32[256,1024]{1,0:T(8,128)S(1)}, f32[256,1024]{1,0:T(8,128)}, u32[]{:S(2)}) copy-start(f32[256,1024]{1,0:T(8,128)} %convolution_add_fusion.2) | copy-start | bytes 3145732
  105.2 1.5 copy-start.3
  105.3 1.5 copy-start.10
  105.6 1.5 copy-start.7
  162.5 4.6 %copy-start.14 = (f32[3]{0:T(128)}, f32[3]{0:T(128)S(1)}, u32[]{:S(2)}) copy-start(f32[3]{0:T(128)S(1)} %get-tuple-element.24) | copy-start | bytes 40
  163.1 4.1 %copy-start.8 = (f32[256,1024]{1,0:T(8,128)S(1)}, f32[256,1024]{1,0:T(8,128)}, u32[]{:S(2)}) copy-start(f32[256,1024]{1,0:T(8,128)} %fusion.51) | copy-start | bytes 3145732
  163.1 4.1 %copy-start.15 = (f32[256,256]{1,0:T(8,128)S(1)}, f32[256,256]{1,0:T(8,128)}, u32[]{:S(2)}) copy-start(f32[256,256]{1,0:T(8,128)} %get-tuple-element.53) | copy-start | bytes 786436
  (1 other events, 0.8 us)
Sparse Core Ops, SparseCore 0:
  10.7 25.2 all-gather.1
where the time goes:
time: 179 us
  waiting for transfers between devices  48.6 us (27%)
  blocking collectives  39.1 us (22%)
  matrix products  36.1 us (20%)
  other arithmetic  20.3 us (11%)
  between operations  17.4 us (10%)
  starting transfers between devices  15.7 us (9%)
    psum x1, blocking collectives, per_device(): gain_total, summary_total = lax.psum((gain_part, summary), ('dp', 'rep'))  39.1 us
    ppermute x4, waiting for transfers between devices, shifted(): return lax.ppermute(value, axis, pairs)  24.2 us
    dot_general x5, matrix products, transposed_product(): lax.dot_general(left, right, (((0,), (0,)), ((), ())), preferred_element_...  12.3 us
    add x1, other arithmetic, per_device(): summary + jnp.stack([jnp.sum(weights * (scores - bias_value)), jnp.sum(we...  11.1 us
    ppermute x4, starting transfers between devices, shifted(): return lax.ppermute(value, axis, pairs)  11 us
    ppermute x1, waiting for transfers between devices, per_device(): circ3 = lax.ppermute(jnp.where(even, circ2, circ4), 'dp', swap)  10 us
    dot_general x5, matrix products, score_tile(): lax.dot_general(circ_block, rec_block, (((1,), (1,)), ((), ())), preferre...  8.68 us
    ppermute x1, waiting for transfers between devices, per_device(): rec1 = lax.ppermute(jnp.where(even, rec2, rec_emb), 'dp', swap)  8.29 us
  transfers between devices with their start and end apart: 9, of which 7 were waited for; matrix products, arithmetic and copies ran while one was open for 17% of the time, Pallas kernels for 0%

commit v1 on v0

--- a/solution.py
+++ b/solution.py
@@ -113,7 +113,7 @@
     ) / rec_length
     grad_records = grad_pre * record_gain
     gain_part = jnp.sum(records.astype(jnp.float32) * grad_pre, axis=0)
-    gain_total, summary_total = lax.psum((gain_part, summary), ("dp", "rep"))
+    gain_total, summary_total = lax.psum(lax.psum((gain_part, summary), "rep"), "dp")
     pair_total = pair_rows * loop_count * rep_count
     statistics = jnp.stack([summary_total[0], summary_total[1]])
     mean_loss = jnp.stack([summary_total[2] / pair_total])

time: 179 us -> 167 us (0.933)
  blocking collectives: 39.1 us -> 26.5 us
    psum x1 -> x2, blocking collectives: 39.1 us -> 26.5 us  [the longest x1 20.7 us: per_device(): lax.psum(lax.psum((gain_part, summary), 'rep'), 'dp')]
  transfers between devices with their start and end apart: 9 -> 9, of which waited for: 7 -> 7; matrix products, arithmetic and copies ran while one was open for 17% -> 18% of each run, Pallas kernels for 0% -> 0%
where the time goes in v1:
time: 167 us; the launch traced here: 166 us
  waiting for transfers between devices  48.6 us (29%)
  matrix products  36.1 us (22%)
  blocking collectives  26.5 us (16%)
  other arithmetic  20.3 us (12%)
  between operations  17.4 us (10%)
  starting transfers between devices  15.7 us (9%)
    ppermute x4, waiting for transfers between devices, shifted(): return lax.ppermute(value, axis, pairs)  24.2 us
    psum x1, blocking collectives, per_device(): lax.psum(lax.psum((gain_part, summary), 'rep'), 'dp')  20.7 us
    dot_general x5, matrix products, transposed_product(): lax.dot_general(left, right, (((0,), (0,)), ((), ())), preferred_element_...  12.3 us
    add x1, other arithmetic, per_device(): summary + jnp.stack([jnp.sum(weights * (scores - bias_value)), jnp.sum(we...  11.1 us
    ppermute x4, starting transfers between devices, shifted(): return lax.ppermute(value, axis, pairs)  11 us
    ppermute x1, waiting for transfers between devices, per_device(): circ3 = lax.ppermute(jnp.where(even, circ2, circ4), 'dp', swap)  10 us
    dot_general x5, matrix products, score_tile(): lax.dot_general(circ_block, rec_block, (((1,), (1,)), ((), ())), preferre...  8.68 us
    ppermute x1, waiting for transfers between devices, per_device(): rec1 = lax.ppermute(jnp.where(even, rec2, rec_emb), 'dp', swap)  8.29 us
  transfers between devices with their start and end apart: 9, of which 7 were waited for; matrix products, arithmetic and copies ran while one was open for 18% of the time, Pallas kernels for 0%

profile of v1, /device:TPU:0, one launch (start us, length us, event | category | flops | bytes accessed | tf_op | source)
XLA Modules:
  0.0 166.0 jit_solution(106100266629176088)
XLA Ops:
  8.6 2.0 %fusion.84 = bf16[256,1024]{1,0:T(8,128)(2,1)} fusion(f32[256]{0:T(256)S(1)} %add_sqrt_fusion, f32[1024]{0:T(1024)} %param.8, bf16[256,1024]{1,0:T(8,128)(2,1)} %param.7), kind=kLoop, calls=%fused_computation.140 | loop fusion | flops 1048576 | bytes 1053696 | tf_op jit(solution)/shard_map/convert_element_type | solution.py:65
  10.6 5.1 %collective-permute-start = (bf16[256,1024]{1,0:T(8,128)(2,1)}, bf16[256,1024]{1,0:T(8,128)(2,1)}, u32[]{:S(2)}, u32[]{:S(2)}) collective-permute-start(bf16[256,1024]{1,0:T(8,128)(2,1)} %fusion.84), channel_id=1, source_target_pairs={{0,24},{4,28},{8,0},{12,4},{16,8},{20,12},{24,16},{28,20},{1,25},{... | collective-permute-start | bytes 1572872 | tf_op jit(solution)/shard_map/ppermute | solution.py:13
  20.5 7.8 %collective-permute-done = bf16[256,1024]{1,0:T(8,128)(2,1)} collective-permute-done((bf16[256,1024]{1,0:T(8,128)(2,1)}, bf16[256,1024]{1,0:T(8,128)(2,1)}, u32[]{:S(2)}, u32[]{:S(2)}) %collective-permute-start) | collective-permute-done | bytes 524320 | tf_op jit(solution)/shard_map/ppermute | solution.py:13
  28.4 4.3 %collective-permute-start.2 = (bf16[256,1024]{1,0:T(8,128)(2,1)}, bf16[256,1024]{1,0:T(8,128)(2,1)}, u32[]{:S(2)}, u32[]{:S(2)}) collective-permute-start(bf16[256,1024]{1,0:T(8,128)(2,1)} %collective-permute-done), channel_id=1, source_target_pairs={{0,24},{4,28},{8,0},{12,4},{16,8},{20,12},{24,16},{28,20},{1,25},{... | collective-permute-start | bytes 1572872 | tf_op jit(solution)/shard_map/ppermute | solution.py:13
  32.6 7.8 %collective-permute-done.4 = bf16[256,1024]{1,0:T(8,128)(2,1)S(1)} collective-permute-done((bf16[256,1024]{1,0:T(8,128)(2,1)S(1)}, bf16[256,1024]{1,0:T(8,128)(2,1)S(1)}, u32[]{:S(2)}, u32[]{:S(2)}) %collective-permute-start.4) | collective-permute-done | bytes 524320 | tf_op jit(solution)/shard_map/ppermute | solution.py:13
  42.0 3.1 %convolution_add_fusion.2 = f32[256,1024]{1,0:T(8,128)} fusion(f32[256,1024]{1,0:T(8,128)} %fusion.68, bf16[256,1024]{1,0:T(8,128)(2,1)S(1)} %collective-permute-done.4, bf16[256,1024]{1,0:T(8,128)(2,1)S(1)} %copy-done, f32[]{:T(128)} %bitcast.69, f32[]{:T(128)} %bitcast), kind=kOutput, calls=%fused_computation.5 | convolution fusion | flops 269090816 | bytes 3145736 | tf_op jit(solution)/shard_map/dot_general | solution.py:23
  45.1 2.2 %multiply_reduce_fusion.7 = (f32[]{:T(128)}, f32[]{:T(128)}, f32[]{:T(128)}, f32[256,256]{1,0:T(8,128)S(1)}) fusion(f32[]{:T(128)} %bitcast.74, f32[]{:T(128)} %bitcast, bf16[256,1024]{1,0:T(8,128)(2,1)S(1)} %fusion.83, bf16[256,1024]{1,0:T(8,128)(2,1)} %collective-permute-done), kind=kOutput, calls=%fused_computation.94 | convolution fusion | flops 135266304 | bytes 1310740 | tf_op jit(solution)/shard_map/dot_general | solution.py:29
  47.3 2.4 %convolution_add_fusion.5 = f32[256,1024]{1,0:T(8,128)} fusion(f32[256,1024]{1,0:T(8,128)S(1)} %fusion.70, bf16[256,1024]{1,0:T(8,128)(2,1)} %collective-permute-done, f32[256,256]{1,0:T(8,128)S(1)} %get-tuple-element.57), kind=kOutput, calls=%fused_computation.11 | convolution fusion | flops 134742016 | bytes 2883584 | tf_op jit(solution)/shard_map/dot_general | solution.py:89
  49.7 1.9 %collective-permute-done.2 = bf16[256,1024]{1,0:T(8,128)(2,1)} collective-permute-done((bf16[256,1024]{1,0:T(8,128)(2,1)}, bf16[256,1024]{1,0:T(8,128)(2,1)}, u32[]{:S(2)}, u32[]{:S(2)}) %collective-permute-start.2) | collective-permute-done | bytes 524320 | tf_op jit(solution)/shard_map/ppermute | solution.py:13
  55.3 6.6 %collective-permute-done.6 = bf16[256,1024]{1,0:T(8,128)(2,1)} collective-permute-done((bf16[256,1024]{1,0:T(8,128)(2,1)S(1)}, bf16[256,1024]{1,0:T(8,128)(2,1)}, u32[]{:S(2)}, u32[]{:S(2)}) %collective-permute-start.6) | collective-permute-done | bytes 524320 | tf_op jit(solution)/shard_map/ppermute | solution.py:13
  63.0 2.6 %collective-permute-start.7 = (bf16[256,1024]{1,0:T(8,128)(2,1)S(1)}, bf16[256,1024]{1,0:T(8,128)(2,1)S(1)}, u32[]{:S(2)}, u32[]{:S(2)}) collective-permute-start(bf16[256,1024]{1,0:T(8,128)(2,1)S(1)} %get-tuple-element.30), channel_id=1, source_target_pairs={{0,4},{4,0},{8,12},{12,8},{16,20},{20,16},{24,28},{28,24},{1,5},{5... | collective-permute-start | bytes 1572872 | tf_op jit(solution)/shard_map/ppermute | solution.py:77
  65.6 2.9 %multiply_reduce_fusion.5 = (f32[]{:T(128)}, f32[]{:T(128)}, f32[]{:T(128)}, f32[256,256]{1,0:T(8,128)}) fusion(f32[]{:T(128)} %bitcast.72, f32[]{:T(128)} %bitcast, bf16[256,1024]{1,0:T(8,128)(2,1)S(1)} %copy-done.6, bf16[256,1024]{1,0:T(8,128)(2,1)} %collective-permute-done.2), kind=kOutput, calls=%fused_computation.92 | convolution fusion | flops 135266304 | bytes 1310740 | tf_op jit(solution)/shard_map/dot_general | solution.py:29
  71.0 8.3 %collective-permute-done.1 = bf16[256,1024]{1,0:T(8,128)(2,1)S(1)} collective-permute-done((bf16[256,1024]{1,0:T(8,128)(2,1)S(1)}, bf16[256,1024]{1,0:T(8,128)(2,1)S(1)}, u32[]{:S(2)}, u32[]{:S(2)}) %collective-permute-start.1) | collective-permute-done | bytes 524320 | tf_op jit(solution)/shard_map/ppermute | solution.py:74
  80.5 10.0 %collective-permute-done.7 = bf16[256,1024]{1,0:T(8,128)(2,1)S(1)} collective-permute-done((bf16[256,1024]{1,0:T(8,128)(2,1)S(1)}, bf16[256,1024]{1,0:T(8,128)(2,1)S(1)}, u32[]{:S(2)}, u32[]{:S(2)}) %collective-permute-start.7) | collective-permute-done | bytes 524320 | tf_op jit(solution)/shard_map/ppermute | solution.py:77
  91.3 3.1 %fusion.37 = f32[256,1024]{1,0:T(8,128)} fusion(bf16[256,1024]{1,0:T(8,128)(2,1)} %copy-done.13, bf16[256,1024]{1,0:T(8,128)(2,1)S(1)} %copy-done, f32[]{:T(128)} %bitcast.76, f32[]{:T(128)} %bitcast), kind=kOutput, calls=%fused_computation.58 | convolution fusion | flops 268828672 | bytes 2097160 | tf_op jit(solution)/shard_map/dot_general | solution.py:23
  94.4 6.1 %collective-permute-done.5 = bf16[256,1024]{1,0:T(8,128)(2,1)S(1)} collective-permute-done((bf16[256,1024]{1,0:T(8,128)(2,1)}, bf16[256,1024]{1,0:T(8,128)(2,1)S(1)}, u32[]{:S(2)}, u32[]{:S(2)}) %collective-permute-start.5) | collective-permute-done | bytes 524320 | tf_op jit(solution)/shard_map/ppermute | solution.py:75
  100.5 1.9 %convolution_add_fusion.1 = f32[256,1024]{1,0:T(8,128)} fusion(f32[256,1024]{1,0:T(8,128)S(1)} %copy-done.4, bf16[256,1024]{1,0:T(8,128)(2,1)S(1)} %collective-permute-done.5, bf16[256,1024]{1,0:T(8,128)(2,1)S(1)} %copy-done, f32[]{:T(128)} %bitcast.68, f32[]{:T(128)} %bitcast), kind=kOutput, calls=%fused_computation.4 | convolution fusion | flops 269090816 | bytes 3145736 | tf_op jit(solution)/shard_map/dot_general | solution.py:23
  102.4 2.9 %multiply_reduce_fusion.1 = (f32[256]{0:T(256)S(1)}, f32[256,1024]{1,0:T(8,128)S(1)}) fusion(f32[256]{0:T(256)S(1)} %add_sqrt_fusion, f32[1024]{0:T(1024)S(1)} %copy-done.11, bf16[256,1024]{1,0:T(8,128)(2,1)S(1)} %copy-done.1, f32[256,1024]{1,0:T(8,128)} %fusion.37, f32[256,1024]{1,0:T(8,128)} %convolution_add_fusion.1, ...), kind=kOutput, calls=%fused_computation.66 | convolution fusion | flops 270925568 | bytes 4724744 | tf_op jit(solution)/shard_map/dot_general | solution.py:23
  107.1 5.2 %multiply_reduce_fusion = (f32[]{:T(128)}, f32[]{:T(128)}, f32[]{:T(128)}, f32[256,1024]{1,0:T(8,128)S(1)}) fusion(f32[]{:T(128)} %bitcast.70, s32[256]{0:T(256)S(1)} %bitcast.106, s32[256]{0:T(256)S(1)} %bitcast.108, s32[256]{0:T(256)S(1)} %bitcast.80, s32[256]{0:T(256)S(1)} %bitcast.82, s32[256]{0:T(256)S(1)} %bitcast.84, s32[256]{0:T(256)S(1)} %bitcast.86, ...), kind=kOutput, calls=%fused_computation.64 | convolution fusion | flops 553910272 | bytes 3690516 | tf_op jit(solution)/shard_map/dot_general | solution.py:50
  112.3 11.1 %fusion.74 = f32[3]{0:T(128)S(1)} fusion(f32[1]{0:T(128)} %bitcast.32, f32[1]{0:T(128)} %bitcast.31, f32[1]{0:T(128)} %bitcast.30, f32[1]{0:T(128)} %bitcast.35, f32[1]{0:T(128)} %bitcast.34, f32[1]{0:T(128)} %bitcast.33, f32[1]{0:T(128)} %bitcast.29, f32[1]{0:T(128)} %bitcast.28, f32[1]{0:T(128)} %bitcast.27, f32[1]{0:T(128)} %bitcast.26, f32[1]{0:T(128)} %bitcast.25, ...), kind=kLoop, calls=%fused_computation.130 | loop fusion | flops 51 | bytes 84 | tf_op jit(solution)/shard_map/add | solution.py:99
  123.4 5.8 %all-reduce.1 = (f32[1024]{0:T(1024)S(1)}, f32[3]{0:T(128)S(1)}) all-reduce(f32[1024]{0:T(1024)S(1)} %get-tuple-element.27, f32[3]{0:T(128)S(1)} %fusion.74), channel_id=1, replica_groups=mesh['dp'=8,'rep'=4] {'rep'}, use_global_device_ids=true, to_apply=%region_5.6 | all-reduce | flops 1027 | bytes 8216 | tf_op jit(solution)/shard_map/psum | solution.py:116
  129.1 20.7 %all-reduce = (f32[1024]{0:T(1024)}, f32[3]{0:T(128)S(1)}) all-reduce(f32[1024]{0:T(1024)S(1)} %get-tuple-element.25, f32[3]{0:T(128)S(1)} %get-tuple-element.26), channel_id=1, replica_groups=mesh['dp'=8,'rep'=4] {'dp'}, use_global_device_ids=true, to_apply=%region_6.7 | all-reduce | flops 1027 | bytes 8216 | tf_op jit(solution)/shard_map/psum | solution.py:116
  150.4 4.0 %fusion.43 = f32[256,1024]{1,0:T(8,128)S(1)} fusion(bf16[1024,1024]{1,0:T(8,128)(2,1)} %all-gather.2.cloned.1.call-done, f32[256,1024]{1,0:T(8,128)S(1)} %get-tuple-element.54, s32[1024]{0:T(1024)S(1)} %iota_add_fusion, s32[256]{0:T(256)S(1)} %bitcast.107, s32[256]{0:T(256)S(1)} %bitcast.109, s32[256]{0:T(256)S(1)} %bitcast.81, s32[256]{0:T(256)S(1)} %bitcast.83, ...), kind=kOutput, calls=%fused_computation.77 | convolution fusion | flops 551026688 | bytes 4214784 | tf_op jit(solution)/shard_map/dot_general | solution.py:98
  154.5 1.6 multiply_reduce_fusion.2
  (61 shorter events, 19.2 us)
Async XLA Ops:
  7.2 8.6 %copy-start.2 = (bf16[256,1024]{1,0:T(8,128)(2,1)S(1)}, bf16[256,1024]{1,0:T(8,128)(2,1)}, u32[]{:S(2)}) copy-start(bf16[256,1024]{1,0:T(8,128)(2,1)} %param.6) | copy-start | bytes 1572868
  7.2 9.7 %copy-start.12 = (s32[256,16]{0,1:T(8,128)S(1)}, s32[256,16]{0,1:T(8,128)}, u32[]{:S(2)}) copy-start(s32[256,16]{0,1:T(8,128)} %param.11) | copy-start | bytes 49156
  7.2 99.9 %all-gather.2.cloned.1.call-start = ((), (), s32[]{:S(2)}) async-start(), calls=%async_computation | async-start | bytes 2621440 | tf_op jit(solution)/shard_map/all_gather | solution.py:81
  10.6 7.1 %copy-start = (bf16[256,1024]{1,0:T(8,128)(2,1)S(1)}, bf16[256,1024]{1,0:T(8,128)(2,1)}, u32[]{:S(2)}) copy-start(bf16[256,1024]{1,0:T(8,128)(2,1)} %fusion.84) | copy-start | bytes 1572868
  10.6 17.7 %collective-permute-start = (bf16[256,1024]{1,0:T(8,128)(2,1)}, bf16[256,1024]{1,0:T(8,128)(2,1)}, u32[]{:S(2)}, u32[]{:S(2)}) collective-permute-start(bf16[256,1024]{1,0:T(8,128)(2,1)} %fusion.84), channel_id=1, source_target_pairs={{0,24},{4,28},{8,0},{12,4},{16,8},{20,12},{24,16},{28,20},{1,25},{... | collective-permute-start | bytes 1572872 | tf_op jit(solution)/shard_map/ppermute | solution.py:13
  16.1 28.9 %copy-start.5 = (bf16[256,1024]{1,0:T(8,128)(2,1)}, bf16[256,1024]{1,0:T(8,128)(2,1)S(1)}, u32[]{:S(2)}) copy-start(bf16[256,1024]{1,0:T(8,128)(2,1)S(1)} %fusion.83) | copy-start | bytes 1572868
  16.2 24.3 %collective-permute-start.4 = (bf16[256,1024]{1,0:T(8,128)(2,1)S(1)}, bf16[256,1024]{1,0:T(8,128)(2,1)S(1)}, u32[]{:S(2)}, u32[]{:S(2)}) collective-permute-start(bf16[256,1024]{1,0:T(8,128)(2,1)S(1)} %fusion.83), channel_id=1, source_target_pairs={{0,8},{4,12},{8,16},{12,20},{16,24},{20,28},{24,0},{28,4},{1,9},{5... | collective-permute-start | bytes 1572872 | tf_op jit(solution)/shard_map/ppermute | solution.py:13
  28.4 23.2 %collective-permute-start.2 = (bf16[256,1024]{1,0:T(8,128)(2,1)}, bf16[256,1024]{1,0:T(8,128)(2,1)}, u32[]{:S(2)}, u32[]{:S(2)}) collective-permute-start(bf16[256,1024]{1,0:T(8,128)(2,1)} %collective-permute-done), channel_id=1, source_target_pairs={{0,24},{4,28},{8,0},{12,4},{16,8},{20,12},{24,16},{28,20},{1,25},{... | collective-permute-start | bytes 1572872 | tf_op jit(solution)/shard_map/ppermute | solution.py:13
  40.4 21.4 %collective-permute-start.6 = (bf16[256,1024]{1,0:T(8,128)(2,1)S(1)}, bf16[256,1024]{1,0:T(8,128)(2,1)}, u32[]{:S(2)}, u32[]{:S(2)}) collective-permute-start(bf16[256,1024]{1,0:T(8,128)(2,1)S(1)} %collective-permute-done.4), channel_id=1, source_target_pairs={{0,8},{4,12},{8,16},{12,20},{16,24},{20,28},{24,0},{28,4},{1,9},{5... | collective-permute-start | bytes 1572872 | tf_op jit(solution)/shard_map/ppermute | solution.py:13
  47.3 4.3 %copy-start.1 = (bf16[256,1024]{1,0:T(8,128)(2,1)S(1)}, bf16[256,1024]{1,0:T(8,128)(2,1)}, u32[]{:S(2)}) copy-start(bf16[256,1024]{1,0:T(8,128)(2,1)} %param.7) | copy-start | bytes 1572868
  47.3 4.3 %copy-start.11 = (f32[1024]{0:T(1024)S(1)}, f32[1024]{0:T(1024)}, u32[]{:S(2)}) copy-start(f32[1024]{0:T(1024)} %param.8) | copy-start | bytes 12292
  49.7 16.0 %copy-start.6 = (bf16[256,1024]{1,0:T(8,128)(2,1)S(1)}, bf16[256,1024]{1,0:T(8,128)(2,1)}, u32[]{:S(2)}) copy-start(bf16[256,1024]{1,0:T(8,128)(2,1)} %copy-done.5) | copy-start | bytes 1572868
  53.2 15.4 %collective-permute-start.3 = (bf16[256,1024]{1,0:T(8,128)(2,1)S(1)}, bf16[256,1024]{1,0:T(8,128)(2,1)S(1)}, u32[]{:S(2)}, u32[]{:S(2)}) collective-permute-start(bf16[256,1024]{1,0:T(8,128)(2,1)S(1)} %get-tuple-element.32), channel_id=1, source_target_pairs={{0,4},{4,0},{8,12},{12,8},{16,20},{20,16},{24,28},{28,24},{1,5},{5... | collective-permute-start | bytes 1572872 | tf_op jit(solution)/shard_map/ppermute | solution.py:76
  54.6 24.7 %collective-permute-start.1 = (bf16[256,1024]{1,0:T(8,128)(2,1)S(1)}, bf16[256,1024]{1,0:T(8,128)(2,1)S(1)}, u32[]{:S(2)}, u32[]{:S(2)}) collective-permute-start(bf16[256,1024]{1,0:T(8,128)(2,1)S(1)} %get-tuple-element.31), channel_id=1, source_target_pairs={{0,4},{4,0},{8,12},{12,8},{16,20},{20,16},{24,28},{28,24},{1,5},{5... | collective-permute-start | bytes 1572872 | tf_op jit(solution)/shard_map/ppermute | solution.py:74
  63.0 27.5 %collective-permute-start.7 = (bf16[256,1024]{1,0:T(8,128)(2,1)S(1)}, bf16[256,1024]{1,0:T(8,128)(2,1)S(1)}, u32[]{:S(2)}, u32[]{:S(2)}) collective-permute-start(bf16[256,1024]{1,0:T(8,128)(2,1)S(1)} %get-tuple-element.30), channel_id=1, source_target_pairs={{0,4},{4,0},{8,12},{12,8},{16,20},{20,16},{24,28},{28,24},{1,5},{5... | collective-permute-start | bytes 1572872 | tf_op jit(solution)/shard_map/ppermute | solution.py:77
  65.6 34.9 %collective-permute-start.5 = (bf16[256,1024]{1,0:T(8,128)(2,1)}, bf16[256,1024]{1,0:T(8,128)(2,1)S(1)}, u32[]{:S(2)}, u32[]{:S(2)}) collective-permute-start(bf16[256,1024]{1,0:T(8,128)(2,1)} %get-tuple-element.29), channel_id=1, source_target_pairs={{0,4},{4,0},{8,12},{12,8},{16,20},{20,16},{24,28},{28,24},{1,5},{5... | collective-permute-start | bytes 1572872 | tf_op jit(solution)/shard_map/ppermute | solution.py:75
  79.3 1.2 copy-start.9
  80.5 20.0 %copy-start.4 = (f32[256,1024]{1,0:T(8,128)S(1)}, f32[256,1024]{1,0:T(8,128)}, u32[]{:S(2)}) copy-start(f32[256,1024]{1,0:T(8,128)} %convolution_add_fusion.2) | copy-start | bytes 3145732
  105.2 1.5 copy-start.3
  105.3 1.5 copy-start.10
  105.6 1.5 copy-start.7
  149.8 4.6 %copy-start.14 = (f32[3]{0:T(128)}, f32[3]{0:T(128)S(1)}, u32[]{:S(2)}) copy-start(f32[3]{0:T(128)S(1)} %get-tuple-element.24) | copy-start | bytes 40
  150.4 4.1 %copy-start.8 = (f32[256,1024]{1,0:T(8,128)S(1)}, f32[256,1024]{1,0:T(8,128)}, u32[]{:S(2)}) copy-start(f32[256,1024]{1,0:T(8,128)} %fusion.51) | copy-start | bytes 3145732
  150.4 4.1 %copy-start.15 = (f32[256,256]{1,0:T(8,128)S(1)}, f32[256,256]{1,0:T(8,128)}, u32[]{:S(2)}) copy-start(f32[256,256]{1,0:T(8,128)} %get-tuple-element.55) | copy-start | bytes 786436
  (1 other events, 0.8 us)
Sparse Core Ops, SparseCore 0:
  10.7 25.2 all-gather.1
